TPU v7x, 256 devices: a whole 4x4x8 slice. The times are simulated.
256 devices in a mesh: term: 8 (over y, core), pass: 32 (over x, z).
Axes of the slice: x: 4, y: 4, z: 8, core: 2. Of those that a mesh axis runs over, the one named last changes fastest.
Arguments:
- hidden: bfloat16 [16384, 4096], P('pass', 'term'), may hold values from -16 to 16
- head_weight: bfloat16 [4096, 16384], P('pass', 'term'), may hold values from -0.09375 to 0.09375
- lengths: int32 [256], P('pass'), may hold values from 1 to 64, as said below
Outputs:
- postings: bfloat16 [16384, 256], P(('term', 'pass'))
Inputs may be any that keep to these rules, and one draw needn't show every extreme that they name: Passage p's valid tokens are its first lengths[p] slots; some passage has exactly 64.
All inputs are finite; a program needn't handle non-finite values.
Results may differ from a plain program's by a relative error of at most 0.013.
Values may be sent and summed in bfloat16 or wider, within the bound.
No kernel may reach another device: no remote copies, remote signals or barrier semaphores. Data moves between devices by JAX's collectives and lax.ppermute only.
A program may use at most 64 MiB of HBM per device.

v0:
```python
import jax
import jax.numpy as jnp
from jax import lax
from jax.sharding import PartitionSpec as P


def body(hidden, head_weight, lengths):
    gathered = lax.all_gather(hidden, "term", axis=1, tiled=True)
    passages = lengths.shape[0]
    tokens_per = gathered.shape[0] // passages
    slab_cols = head_weight.shape[1]
    allowed = jnp.arange(tokens_per, dtype=jnp.int32)[None, :] < lengths[:, None]
    logits = jnp.dot(
        gathered,
        lax.all_gather(head_weight, "pass", axis=0, tiled=True),
        preferred_element_type=jnp.float32,
    )
    impacts = jnp.log1p(jnp.maximum(logits, jnp.float32(0.0)))
    impacts = impacts.reshape(passages, tokens_per, slab_cols)
    impacts = jnp.where(allowed[:, :, None], impacts, jnp.float32(0.0))
    pooled = jnp.max(impacts, axis=1).astype(jnp.bfloat16)
    owners = lax.axis_size("pass")
    range_cols = slab_cols // owners
    local_max = jnp.max(pooled.astype(jnp.float32), axis=0)
    column_max = lax.pmax(local_max, "pass")
    payload = (pooled.astype(jnp.float32) / (1.0 + column_max)[None, :]).astype(jnp.bfloat16)
    shaped = payload.reshape(passages, owners, range_cols)
    return jnp.transpose(
        lax.all_to_all(shaped, "pass", split_axis=1, concat_axis=0, tiled=True)[:, 0, :]
    )


def solution(mesh):
    return jax.shard_map(
        body,
        mesh=mesh,
        in_specs=(P("pass", "term"), P("pass", "term"), P("pass")),
        out_specs=P(("term", "pass"), None),
        check_vma=False,
    )
```

profile of v0, /device:TPU:8, one launch (start us, length us, event | category | flops | bytes accessed | tf_op | source)
XLA Modules:
  0.0 297.9 jit_solution(6542916140701454250)
XLA Ops:
  6.5 0.0 all-gather.3.cloned.1.call-start
  6.5 0.7 all-gather.3.cloned.1.call-update
  7.3 0.0 all-gather.5.cloned.1.call-start
  7.3 0.7 all-gather.5.cloned.1.call-update
  8.0 0.7 iota_compare_fusion
  8.7 37.0 %all-gather.3.cloned.1.call-done = bf16[512,4096]{1,0:T(8,128)(2,1)} async-done(((bf16[512,512]{1,0:T(8,128)(2,1)}), bf16[512,4096]{1,0:T(8,128)(2,1)}) %all-gather.3.cloned.1.call-update) | async-done | bytes 4194320 | tf_op jit(solution)/shard_map/all_gather | solution.py:8
  45.8 144.1 %all-gather.5.cloned.1.call-done = bf16[4096,2048]{1,0:T(8,128)(2,1)} async-done(((bf16[128,2048]{1,0:T(8,128)(2,1)}), bf16[4096,2048]{1,0:T(8,128)(2,1)}) %all-gather.5.cloned.1.call-update) | async-done | bytes 16777232 | tf_op jit(solution)/shard_map/all_gather | solution.py:15
  189.9 14.8 %select_reduce_fusion = bf16[8,2048]{1,0:T(8,128)(2,1)S(1)} fusion(pred[8,64]{1,0:T(8,128)(4,1)S(1)} %iota_compare_fusion, bf16[512,4096]{1,0:T(8,128)(2,1)} %all-gather.3.cloned.1.call-done, bf16[4096,2048]{1,0:T(8,128)(2,1)} %all-gather.5.cloned.1.call-done), kind=kOutput, calls=%fused_computation | convolution fusion | flops 8594112512 | bytes 21004800 | tf_op jit(solution)/shard_map/dot_general | solution.py:13
  204.8 0.1 reshape.37
  204.9 72.3 %pmax.7 = f32[2048]{0:T(1024)S(1)} all-reduce(bf16[2048]{0:T(1024)(128)(2,1)S(1)} %convert_reduce_fusion), channel_id=1, replica_groups=mesh['term'=8,'pass'=32] {'pass'}, use_global_device_ids=true, to_apply=%region_2.3 | all-reduce | flops 2048 | bytes 12288 | tf_op jit(solution)/shard_map/pmax | solution.py:25
  277.2 0.1 div.11
  277.3 0.1 reshape.38
  277.4 12.8 %all_to_all.15 = bf16[32,2,256]{2,1,0:T(2,128)(2,1)S(1)} all-to-all(bf16[32,2,256]{2,1,0:T(2,128)(2,1)S(1)} %reshape.38), channel_id=1, replica_groups=mesh['term'=8,'pass'=32] {'pass'}, dimensions={0} | all-to-all | bytes 65536 | tf_op jit(solution)/shard_map/all_to_all | solution.py:29
  290.2 0.1 reshape.39
  290.4 0.7 copy.7
  (5 shorter events, 0.1 us)
Async XLA Ops:
  6.5 39.2 %all-gather.3.cloned.1.call-start = ((), (), s32[]{:S(2)}) async-start(), calls=%async_computation.1 | async-start | bytes 4718592 | tf_op jit(solution)/shard_map/all_gather | solution.py:8
  7.3 182.6 %all-gather.5.cloned.1.call-start = ((), (), s32[]{:S(2)}) async-start(), calls=%async_computation.2 | async-start | bytes 17301504 | tf_op jit(solution)/shard_map/all_gather | solution.py:15
Sparse Core Ops, SparseCore 0:
  9.2 36.5 all-gather.2
  48.4 141.4 all-gather.4
where the time goes:
time: 298 us
  waiting for transfers between devices  183 us (61%)
  blocking collectives  85.1 us (29%)
  matrix products  14.8 us (5%)
  between operations  13.5 us (5%)
    all_gather x1, waiting for transfers between devices, body(): lax.all_gather(head_weight, 'pass', axis=0, tiled=True)  144 us
    pmax x1, blocking collectives, body(): column_max = lax.pmax(local_max, 'pass')  72.3 us
    all_gather x1, waiting for transfers between devices, body(): gathered = lax.all_gather(hidden, 'term', axis=1, tiled=True)  37 us
    dot_general x1, matrix products, body(): jnp.dot(gathered, lax.all_gather(head_weight, 'pass', axis=0, tiled=True)...  14.8 us
    all_to_all x1, blocking collectives, body(): lax.all_to_all(shaped, 'pass', split_axis=1, concat_axis=0, tiled=True)  12.8 us
  transfers between devices with their start and end apart: 2, of which 2 were waited for; matrix products, arithmetic and copies ran while one was open for 0% of the time, Pallas kernels for 0%

commit v1 on v0

--- a/solution.py
+++ b/solution.py
@@ -5,7 +5,23 @@
 
 
 def body(hidden, head_weight, lengths):
-    gathered = lax.all_gather(hidden, "term", axis=1, tiled=True)
+    peers, index, extent = (lax.axis_size("term"), lax.axis_index("term"), hidden.shape[1])
+    ahead = [(i, (i + 1) % peers) for i in range(peers)]
+    left = [(i, (i - 1) % peers) for i in range(peers)]
+    gathered = jnp.zeros((*hidden.shape[:1], peers * extent, *hidden.shape[1 + 1 :]), hidden.dtype)
+    gathered = lax.dynamic_update_slice_in_dim(gathered, hidden, index * extent, axis=1)
+    from_left = from_right = hidden
+    half = peers // 2
+    for step in range(1, half + 1):
+        from_left = lax.ppermute(from_left, "term", ahead)
+        gathered = lax.dynamic_update_slice_in_dim(
+            gathered, from_left, (index - step) % peers * extent, axis=1
+        )
+        if step < peers - half:
+            from_right = lax.ppermute(from_right, "term", left)
+            gathered = lax.dynamic_update_slice_in_dim(
+                gathered, from_right, (index + step) % peers * extent, axis=1
+            )
     passages = lengths.shape[0]
     tokens_per = gathered.shape[0] // passages
     slab_cols = head_weight.shape[1]

time: 298 us -> 262 us (0.88)
  waiting for transfers between devices: 183 us -> 132 us
  local copies, waits for them, and re-layouts: 1.16 us -> 10.7 us
  starting transfers between devices: 0.04 us -> 5.48 us
    all_gather x1 -> x0, waiting for transfers between devices: 37 us -> none  [body(): gathered = lax.all_gather(hidden, 'term', axis=1, tiled=True)]
    all_gather x1, waiting for transfers between devices: 144 us -> 111 us  [body(): lax.all_gather(head_weight, 'pass', axis=0, tiled=True)]
    ppermute x0 -> x7, waiting for transfers between devices: none -> 20.4 us  [the longest x4 20.4 us: body(): from_left = lax.ppermute(from_left, 'term', ahead)]
    dynamic_update_slice x0 -> x8, local copies, waits for them, and re-layouts: none -> 7.12 us  [the longest x4 3.51 us: body(): lax.dynamic_update_slice_in_dim(gathered, from_left, (index - step) % pee...]
    ppermute x0 -> x7, starting transfers between devices: none -> 5.48 us  [the longest x3 5.46 us: body(): from_right = lax.ppermute(from_right, 'term', left)]
  transfers between devices with their start and end apart: 2 -> 8, of which waited for: 2 -> 5; matrix products, arithmetic and copies ran while one was open for 0% -> 4% of each run, Pallas kernels for 0% -> 0%
where the time goes in v1:
time: 262 us; the launch traced here: 261 us
  waiting for transfers between devices  132 us (50%)
  blocking collectives  85.1 us (32%)
  matrix products  14.8 us (6%)
  between operations  13.5 us (5%)
  local copies, waits for them, and re-layouts  10.7 us (4%)
  starting transfers between devices  5.48 us (2%)
    all_gather x1, waiting for transfers between devices, body(): lax.all_gather(head_weight, 'pass', axis=0, tiled=True)  111 us
    pmax x1, blocking collectives, body(): column_max = lax.pmax(local_max, 'pass')  72.3 us
    ppermute x4, waiting for transfers between devices, body(): from_left = lax.ppermute(from_left, 'term', ahead)  20.4 us
    dot_general x1, matrix products, body(): jnp.dot(gathered, lax.all_gather(head_weight, 'pass', axis=0, tiled=True)...  14.8 us
    all_to_all x1, blocking collectives, body(): lax.all_to_all(shaped, 'pass', split_axis=1, concat_axis=0, tiled=True)  12.8 us
    ppermute x3, starting transfers between devices, body(): from_right = lax.ppermute(from_right, 'term', left)  5.46 us
  transfers between devices with their start and end apart: 8, of which 5 were waited for; matrix products, arithmetic and copies ran while one was open for 4% of the time, Pallas kernels for 0%

profile of v1, /device:TPU:8, one launch (start us, length us, event | category | flops | bytes accessed | tf_op | source)
XLA Modules:
  0.0 261.4 jit_solution(2563005967418677957)
XLA Ops:
  6.5 0.7 all-gather.2.cloned.1.call-update
  7.3 1.7 collective-permute-start.1
  9.0 7.1 %collective-permute-done = bf16[512,512]{1,0:T(8,128)(2,1)S(1)} collective-permute-done((bf16[512,512]{1,0:T(8,128)(2,1)}, bf16[512,512]{1,0:T(8,128)(2,1)S(1)}, u32[]{:S(2)}, u32[]{:S(2)}) %collective-permute-start) | collective-permute-done | bytes 524320 | tf_op jit(solution)/shard_map/ppermute | solution.py:16
  16.1 2.0 collective-permute-start.3
  18.1 6.6 %collective-permute-done.2 = bf16[512,512]{1,0:T(8,128)(2,1)S(1)} collective-permute-done((bf16[512,512]{1,0:T(8,128)(2,1)S(1)}, bf16[512,512]{1,0:T(8,128)(2,1)S(1)}, u32[]{:S(2)}, u32[]{:S(2)}) %collective-permute-start.2) | collective-permute-done | bytes 524320 | tf_op jit(solution)/shard_map/ppermute | solution.py:16
  24.7 2.4 broadcast_in_dim.20
  27.2 0.9 constant_dynamic-update-slice_fusion.7
  28.1 1.7 collective-permute-start.5
  29.8 0.9 constant_dynamic-update-slice_fusion.6
  30.7 2.6 collective-permute-done.4
  33.3 0.9 constant_dynamic-update-slice_fusion.5
  34.2 0.9 constant_dynamic-update-slice_fusion.4
  35.1 0.9 constant_dynamic-update-slice_fusion.3
  35.9 0.9 constant_dynamic-update-slice_fusion.2
  36.8 0.9 constant_dynamic-update-slice_fusion.1
  37.7 4.2 %collective-permute-done.6 = bf16[512,512]{1,0:T(8,128)(2,1)S(1)} collective-permute-done((bf16[512,512]{1,0:T(8,128)(2,1)S(1)}, bf16[512,512]{1,0:T(8,128)(2,1)S(1)}, u32[]{:S(2)}, u32[]{:S(2)}) %collective-permute-start.6) | collective-permute-done | bytes 524320 | tf_op jit(solution)/shard_map/ppermute | solution.py:16
  41.9 0.9 constant_dynamic-update-slice_fusion
  42.8 110.6 %all-gather.2.cloned.1.call-done = bf16[4096,2048]{1,0:T(8,128)(2,1)} async-done(((bf16[128,2048]{1,0:T(8,128)(2,1)}), bf16[4096,2048]{1,0:T(8,128)(2,1)}) %all-gather.2.cloned.1.call-update) | async-done | bytes 16777232 | tf_op jit(solution)/shard_map/all_gather | solution.py:31
  153.4 14.8 %select_reduce_fusion = bf16[8,2048]{1,0:T(8,128)(2,1)S(1)} fusion(pred[8,64]{1,0:T(8,128)(4,1)S(1)} %iota_compare_fusion, bf16[512,4096]{1,0:T(8,128)(2,1)} %constant_dynamic-update-slice_fusion, bf16[4096,2048]{1,0:T(8,128)(2,1)} %all-gather.2.cloned.1.call-done), kind=kOutput, calls=%fused_computation | convolution fusion | flops 8594112512 | bytes 21004800 | tf_op jit(solution)/shard_map/dot_general | solution.py:29
  168.2 0.1 reshape.37
  168.3 72.3 %pmax.7 = f32[2048]{0:T(1024)S(1)} all-reduce(bf16[2048]{0:T(1024)(128)(2,1)S(1)} %convert_reduce_fusion), channel_id=1, replica_groups=mesh['term'=8,'pass'=32] {'pass'}, use_global_device_ids=true, to_apply=%region_2.3 | all-reduce | flops 2048 | bytes 12288 | tf_op jit(solution)/shard_map/pmax | solution.py:41
  240.8 0.1 reshape.38
  240.9 12.8 %all_to_all.15 = bf16[32,2,256]{2,1,0:T(2,128)(2,1)S(1)} all-to-all(bf16[32,2,256]{2,1,0:T(2,128)(2,1)S(1)} %reshape.38), channel_id=1, replica_groups=mesh['term'=8,'pass'=32] {'pass'}, dimensions={0} | all-to-all | bytes 65536 | tf_op jit(solution)/shard_map/all_to_all | solution.py:45
  253.8 0.7 copy.7
  (20 shorter events, 0.4 us)
Async XLA Ops:
  6.5 20.6 %copy-start = (bf16[512,512]{1,0:T(8,128)(2,1)S(1)}, bf16[512,512]{1,0:T(8,128)(2,1)}, u32[]{:S(2)}) copy-start(bf16[512,512]{1,0:T(8,128)(2,1)} %param.3) | copy-start | bytes 1572868
  6.5 21.5 %copy-start.1 = (s32[8]{0:T(128)S(1)}, s32[8]{0:T(128)}, u32[]{:S(2)}) copy-start(s32[8]{0:T(128)} %param.5) | copy-start | bytes 100
  6.5 146.8 %all-gather.2.cloned.1.call-start = ((), (), s32[]{:S(2)}) async-start(), calls=%async_computation.1 | async-start | bytes 17301504 | tf_op jit(solution)/shard_map/all_gather | solution.py:31
  7.3 8.8 %collective-permute-start = (bf16[512,512]{1,0:T(8,128)(2,1)}, bf16[512,512]{1,0:T(8,128)(2,1)S(1)}, u32[]{:S(2)}, u32[]{:S(2)}) collective-permute-start(bf16[512,512]{1,0:T(8,128)(2,1)} %param.3), channel_id=1, source_target_pairs={{0,32},{32,64},{64,96},{96,128},{128,160},{160,192},{192,224},{224... | collective-permute-start | bytes 1572872 | tf_op jit(solution)/shard_map/ppermute | solution.py:16
  7.3 8.8 %collective-permute-start.1 = (bf16[512,512]{1,0:T(8,128)(2,1)}, bf16[512,512]{1,0:T(8,128)(2,1)S(1)}, u32[]{:S(2)}, u32[]{:S(2)}) collective-permute-start(bf16[512,512]{1,0:T(8,128)(2,1)} %param.3), channel_id=1, source_target_pairs={{0,224},{32,0},{64,32},{96,64},{128,96},{160,128},{192,160},{224,1... | collective-permute-start | bytes 1572872 | tf_op jit(solution)/shard_map/ppermute | solution.py:21
  16.1 8.6 %collective-permute-start.2 = (bf16[512,512]{1,0:T(8,128)(2,1)S(1)}, bf16[512,512]{1,0:T(8,128)(2,1)S(1)}, u32[]{:S(2)}, u32[]{:S(2)}) collective-permute-start(bf16[512,512]{1,0:T(8,128)(2,1)S(1)} %collective-permute-done), channel_id=1, source_target_pairs={{0,32},{32,64},{64,96},{96,128},{128,160},{160,192},{192,224},{224... | collective-permute-start | bytes 1572872 | tf_op jit(solution)/shard_map/ppermute | solution.py:16
  16.1 12.1 %collective-permute-start.3 = (bf16[512,512]{1,0:T(8,128)(2,1)S(1)}, bf16[512,512]{1,0:T(8,128)(2,1)S(1)}, u32[]{:S(2)}, u32[]{:S(2)}) collective-permute-start(bf16[512,512]{1,0:T(8,128)(2,1)S(1)} %collective-permute-done.1), channel_id=1, source_target_pairs={{0,224},{32,0},{64,32},{96,64},{128,96},{160,128},{192,160},{224,1... | collective-permute-start | bytes 1572872 | tf_op jit(solution)/shard_map/ppermute | solution.py:21
  24.7 8.6 %collective-permute-start.4 = (bf16[512,512]{1,0:T(8,128)(2,1)S(1)}, bf16[512,512]{1,0:T(8,128)(2,1)S(1)}, u32[]{:S(2)}, u32[]{:S(2)}) collective-permute-start(bf16[512,512]{1,0:T(8,128)(2,1)S(1)} %collective-permute-done.2), channel_id=1, source_target_pairs={{0,32},{32,64},{64,96},{96,128},{128,160},{160,192},{192,224},{224... | collective-permute-start | bytes 1572872 | tf_op jit(solution)/shard_map/ppermute | solution.py:16
  28.1 8.7 %collective-permute-start.5 = (bf16[512,512]{1,0:T(8,128)(2,1)S(1)}, bf16[512,512]{1,0:T(8,128)(2,1)S(1)}, u32[]{:S(2)}, u32[]{:S(2)}) collective-permute-start(bf16[512,512]{1,0:T(8,128)(2,1)S(1)} %collective-permute-done.3), channel_id=1, source_target_pairs={{0,224},{32,0},{64,32},{96,64},{128,96},{160,128},{192,160},{224,1... | collective-permute-start | bytes 1572872 | tf_op jit(solution)/shard_map/ppermute | solution.py:21
  33.3 8.6 %collective-permute-start.6 = (bf16[512,512]{1,0:T(8,128)(2,1)S(1)}, bf16[512,512]{1,0:T(8,128)(2,1)S(1)}, u32[]{:S(2)}, u32[]{:S(2)}) collective-permute-start(bf16[512,512]{1,0:T(8,128)(2,1)S(1)} %collective-permute-done.4), channel_id=1, source_target_pairs={{0,32},{32,64},{64,96},{96,128},{128,160},{160,192},{192,224},{224... | collective-permute-start | bytes 1572872 | tf_op jit(solution)/shard_map/ppermute | solution.py:16
Sparse Core Ops, SparseCore 0:
  10.0 143.3 all-gather.1
